TPU v7x, 32 devices: a whole 2x2x4 slice. The times are simulated.
32 devices in a mesh: gx: 4 (over x, core), yz: 8 (over z, y).
Axes of the slice: x: 2, y: 2, z: 4, core: 2. Of those that a mesh axis runs over, the one named last changes fastest.
Arguments:
- stream: bfloat16 [128, 9216], P('yz', 'gx'), may hold values from -1700 to 1700
- ln_gain: bfloat16 [9216], P('gx'), may hold values from 0.099609375 to 1.8984375
- q_weight: bfloat16 [9216, 12288], P('gx', 'yz'), may hold values from -0.0625 to 0.0625
- kv_weight: bfloat16 [9216, 512], P('gx', 'yz'), may hold values from -0.0625 to 0.0625
- out_weight: bfloat16 [12288, 9216], P('yz', 'gx'), may hold values from -0.0546875 to 0.0546875
- gate_weight: bfloat16 [9216, 36864], P('gx', 'yz'), may hold values from -0.0625 to 0.0625
- up_weight: bfloat16 [9216, 36864], P('gx', 'yz'), may hold values from -0.0625 to 0.0625
- down_weight: bfloat16 [36864, 9216], P('yz', 'gx'), may hold values from -0.03125 to 0.03125
- cache: bfloat16 [128, 1536, 512], P(('gx', 'yz')), may hold values from -620 to 620
- lengths: int32 [128], P(('gx', 'yz')), may hold values from 1 to 1536, as said below
Outputs:
- update: bfloat16 [128, 9216], P('yz', 'gx')
Inputs may be any that keep to these rules, and one draw needn't show every extreme that they name: `lengths`: in every draw some sequence has all 1536 slots filled.
All inputs are finite; a program needn't handle non-finite values.
Results may differ from a plain program's by a relative error of at most 0.0082.
Values may be sent and summed in bfloat16 or wider, within the bound.
A program may use at most 192 MiB of HBM per device.

v0:
```python
import math
import jax
import jax.numpy as jnp
from jax import lax
from jax.sharding import PartitionSpec as P

D = 9216


def attend_local(query, new_kv, cache, lengths):
    seqs = query.shape[0]
    head_dim = cache.shape[2] // 2
    heads = query.shape[1] // head_dim
    query_vectors = query.reshape(seqs, heads, head_dim)
    key_rows = cache[:, :, :head_dim]
    value_rows = cache[:, :, head_dim:]
    new_key = new_kv[:, :head_dim]
    new_value = new_kv[:, head_dim:]
    score_scale = 1.0 / math.sqrt(head_dim)
    attention_logits = (
        jnp.einsum("tgb,twb->tgw", query_vectors, key_rows, preferred_element_type=jnp.float32)
        * score_scale
    )
    own = (
        jnp.einsum("shd,sd->sh", query_vectors, new_key, preferred_element_type=jnp.float32)
        * score_scale
    )
    positions = lax.broadcasted_iota(jnp.int32, (1, 1, cache.shape[1]), 2)
    valid = positions < lengths[:, None, None]
    top = jnp.maximum(jnp.max(jnp.where(valid, attention_logits, own[:, :, None]), axis=2), own)
    weights = jnp.where(valid, jnp.exp(attention_logits - top[:, :, None]), jnp.float32(0.0))
    own_weight = jnp.exp(own - top)
    denom = jnp.sum(weights, axis=2) + own_weight
    attention_probabilities = (weights / denom[:, :, None]).astype(jnp.bfloat16)
    own_prob = (own_weight / denom).astype(jnp.bfloat16)
    value_mixture = jnp.einsum(
        "aqc,acn->aqn", attention_probabilities, value_rows, preferred_element_type=jnp.float32
    )
    value_mixture = (
        value_mixture
        + own_prob.astype(jnp.float32)[:, :, None] * new_value.astype(jnp.float32)[:, None, :]
    )
    return value_mixture.astype(jnp.bfloat16).reshape(seqs, heads * head_dim)


def body(
    stream,
    ln_gain,
    q_weight,
    kv_weight,
    out_weight,
    gate_weight,
    up_weight,
    down_weight,
    cache,
    lengths,
):
    values_f = stream.astype(jnp.float32)
    total, squares = lax.psum(
        (jnp.sum(values_f, axis=1), jnp.sum(values_f * values_f, axis=1)), "gx"
    )
    mean = total / D
    variance = squares / D - mean * mean
    normed = (
        (values_f - mean[:, None])
        * lax.rsqrt(variance + 1e-05)[:, None]
        * ln_gain.astype(jnp.float32)[None, :]
    ).astype(jnp.bfloat16)
    gathered = lax.all_gather(normed, "yz", axis=0, tiled=True)
    query_part = jnp.dot(gathered, q_weight, preferred_element_type=jnp.float32)
    kv_part = jnp.dot(gathered, kv_weight, preferred_element_type=jnp.float32)
    query_block, kv_block = (
        lax.psum_scatter(query_part, "gx", scatter_dimension=0, tiled=True),
        lax.psum_scatter(kv_part, "gx", scatter_dimension=0, tiled=True),
    )
    query_own, kv_own = (
        lax.all_to_all(
            query_block.astype(jnp.bfloat16), "yz", split_axis=0, concat_axis=1, tiled=True
        ),
        lax.all_to_all(
            kv_block.astype(jnp.bfloat16), "yz", split_axis=0, concat_axis=1, tiled=True
        ),
    )
    attended = attend_local(query_own, kv_own, cache, lengths)
    head_block = lax.all_to_all(attended, "yz", split_axis=1, concat_axis=0, tiled=True)
    head_all = lax.all_gather(head_block, "gx", axis=0, tiled=True)
    gate_part = jnp.dot(gathered, gate_weight, preferred_element_type=jnp.float32)
    up_part = jnp.dot(gathered, up_weight, preferred_element_type=jnp.float32)
    gate_share, up_share = (
        lax.psum_scatter(gate_part, "gx", scatter_dimension=0, tiled=True),
        lax.psum_scatter(up_part, "gx", scatter_dimension=0, tiled=True),
    )
    hidden_share = (jax.nn.silu(gate_share) * up_share).astype(jnp.bfloat16)
    hidden = lax.all_gather(hidden_share, "gx", axis=0, tiled=True)
    first = jnp.dot(head_all, out_weight, preferred_element_type=jnp.float32)
    update = lax.psum_scatter(
        first + jnp.dot(hidden, down_weight, preferred_element_type=jnp.float32),
        "yz",
        scatter_dimension=0,
        tiled=True,
    )
    return update.astype(jnp.bfloat16)


def solution(mesh):
    return jax.shard_map(
        body,
        mesh=mesh,
        in_specs=(
            P("yz", "gx"),
            P("gx"),
            P("gx", "yz"),
            P("gx", "yz"),
            P("yz", "gx"),
            P("gx", "yz"),
            P("gx", "yz"),
            P("yz", "gx"),
            P(("gx", "yz"), None, None),
            P(("gx", "yz")),
        ),
        out_specs=P("yz", "gx"),
        check_vma=False,
    )
```

profile of v0, /device:TPU:0, one launch (start us, length us, event | category | flops | bytes accessed | tf_op | source)
XLA Modules:
  0.0 278.6 jit_solution(908472190213945265)
XLA Ops:
  6.5 1.1 convert_reduce_fusion
  7.6 0.7 convert_element_type.37
  8.3 8.3 %all-reduce = (f32[16]{0:T(128)S(1)}, f32[16]{0:T(128)S(1)}) all-reduce(f32[16]{0:T(128)S(1)} %get-tuple-element.6, f32[16]{0:T(128)S(1)} %get-tuple-element.5), channel_id=1, replica_groups=mesh['gx'=4,'yz'=8] {'gx'}, use_global_device_ids=true, to_apply=%region_3.0 | all-reduce | flops 32 | bytes 256 | tf_op jit(solution)/shard_map/psum | solution.py:59
  16.6 1.0 fusion.20
  17.6 32.0 %all_gather.9 = bf16[128,2304]{1,0:T(8,128)(2,1)S(1)} all-gather(bf16[16,2304]{1,0:T(8,128)(2,1)S(1)} %fusion.20), channel_id=1, replica_groups=mesh['gx'=4,'yz'=8] {'yz'}, dimensions={0}, use_global_device_ids=true | all-gather | bytes 663552 | tf_op jit(solution)/shard_map/all_gather | solution.py:69
  49.6 0.9 fusion.29
  50.5 0.0 reduce-scatter.8.cloned.1.call-update
  50.5 0.0 reduce-scatter.6.cloned.1.call-start
  50.6 5.0 %fusion.28 = f32[128,1536]{1,0:T(8,128)} fusion(bf16[128,2304]{1,0:T(8,128)(2,1)S(1)} %all_gather.9, bf16[2304,1536]{1,0:T(8,128)(2,1)} %param.12), kind=kOutput, calls=%fused_computation.38 | convolution fusion | flops 905969664 | bytes 8454144 | tf_op jit(solution)/shard_map/dot_general | solution.py:70
  55.6 0.0 reduce-scatter.6.cloned.1.call-update
  55.6 0.0 reduce-scatter.12.cloned.1.call-start
  55.6 11.4 %fusion.31 = f32[128,4608]{1,0:T(8,128)} fusion(bf16[128,2304]{1,0:T(8,128)(2,1)S(1)} %all_gather.9, bf16[2304,4608]{1,0:T(8,128)(2,1)} %param.16), kind=kOutput, calls=%fused_computation.41 | convolution fusion | flops 2717908992 | bytes 24182784 | tf_op jit(solution)/shard_map/dot_general | solution.py:88
  67.1 0.0 reduce-scatter.12.cloned.1.call-update
  67.1 0.0 reduce-scatter.10.cloned.1.call-start
  67.2 11.4 %fusion.30 = f32[128,4608]{1,0:T(8,128)} fusion(bf16[128,2304]{1,0:T(8,128)(2,1)S(1)} %all_gather.9, bf16[2304,4608]{1,0:T(8,128)(2,1)} %param.15), kind=kOutput, calls=%fused_computation.40 | convolution fusion | flops 2717908992 | bytes 24182784 | tf_op jit(solution)/shard_map/dot_general | solution.py:87
  78.5 0.0 reduce-scatter.10.cloned.1.call-update
  78.6 0.0 reduce-scatter.8.cloned.1.call-done
  78.6 0.7 convert_element_type.40
  79.3 0.7 reshape.47
  80.0 5.4 %all-to-all-start.1 = ((bf16[8,2,128]{2,1,0:T(2,128)(2,1)}), bf16[8,2,128]{2,1,0:T(2,128)(2,1)S(1)}, u32[]{:S(2)}, u32[]{:S(2)}) async-start(bf16[8,2,128]{2,1,0:T(2,128)(2,1)} %reshape.47), calls=%async_computation.3 | async-start | bytes 8192 | tf_op jit(solution)/shard_map/all_to_all | solution.py:80
  85.4 0.1 iota_compare_fusion
  85.4 6.3 %all-to-all-done.1 = bf16[8,2,128]{2,1,0:T(2,128)(2,1)S(1)} async-done(((bf16[8,2,128]{2,1,0:T(2,128)(2,1)}), bf16[8,2,128]{2,1,0:T(2,128)(2,1)S(1)}, u32[]{:S(2)}, u32[]{:S(2)}) %all-to-all-start.1) | async-done | bytes 4128 | tf_op jit(solution)/shard_map/all_to_all | solution.py:80
  91.8 0.1 reshape.48
  91.8 0.1 all_to_all.46
  91.9 4.2 %reduce-scatter.6.cloned.1.call-done = f32[32,1536]{1,0:T(8,128)} async-done(((f32[128,1536]{1,0:T(8,128)}), f32[32,1536]{1,0:T(8,128)}) %reduce-scatter.6.cloned.1.call-update) | async-done | bytes 196624 | tf_op jit(solution)/shard_map/reduce_scatter | solution.py:73
  96.1 0.9 convert_element_type.39
  97.1 0.7 all_to_all.40
  97.7 5.5 %all-to-all-start = ((bf16[8,4,1536]{2,1,0:T(4,128)(2,1)}), bf16[8,4,1536]{2,1,0:T(4,128)(2,1)S(1)}, u32[]{:S(2)}, u32[]{:S(2)}) async-start(bf16[8,4,1536]{2,1,0:T(4,128)(2,1)} %all_to_all.40), calls=%async_computation.1 | async-start | bytes 196608 | tf_op jit(solution)/shard_map/all_to_all | solution.py:77
  103.2 0.0 all-gather.2.cloned.1.call-start
  103.3 7.1 %all-to-all-done = bf16[8,4,1536]{2,1,0:T(4,128)(2,1)S(1)} async-done(((bf16[8,4,1536]{2,1,0:T(4,128)(2,1)}), bf16[8,4,1536]{2,1,0:T(4,128)(2,1)S(1)}, u32[]{:S(2)}, u32[]{:S(2)}) %all-to-all-start) | async-done | bytes 98336 | tf_op jit(solution)/shard_map/all_to_all | solution.py:77
  110.4 0.1 reshape.44
  110.5 0.1 fusion.22
  110.6 21.2 %reduce-scatter.12.cloned.1.call-done = f32[32,4608]{1,0:T(8,128)} async-done(((f32[128,4608]{1,0:T(8,128)}), f32[32,4608]{1,0:T(8,128)}) %reduce-scatter.12.cloned.1.call-update) | async-done | bytes 589840 | tf_op jit(solution)/shard_map/reduce_scatter | solution.py:91
  131.8 35.7 %reduce-scatter.10.cloned.1.call-done = f32[32,4608]{1,0:T(8,128)} async-done(((f32[128,4608]{1,0:T(8,128)}), f32[32,4608]{1,0:T(8,128)}) %reduce-scatter.10.cloned.1.call-update) | async-done | bytes 589840 | tf_op jit(solution)/shard_map/reduce_scatter | solution.py:90
  167.5 2.1 multiply_convert_fusion
  169.6 0.0 all-gather.2.cloned.1.call-update
  169.6 0.0 reduce-scatter.14.cloned.1.call-start
  169.7 3.0 %select_reduce_fusion = (f32[4,48]{1,0:T(4,128)S(1)}, f32[4,48,1536]{2,1,0:T(8,128)S(1)}) fusion(f32[4,48]{1,0:T(4,128)S(1)} %broadcast_multiply_fusion, pred[4,1536]{1,0:T(4,128)(4,1)S(1)} %iota_compare_fusion, bf16[4,48,256]{2,1,0:T(8,128)(2,1)S(1)} %reshape.44, bf16[4,1536,512]{2,1,0:T(8,128)(2,1)} %param.18), kind=kOutput, calls=%fused_computation.8 | convolution fusion | flops 151879488 | bytes 4431360 | tf_op jit(solution)/shard_map/tgb,twb->tgw/dot_general | solution.py:21
  172.7 0.4 fusion.13
  173.1 2.6 fusion.10
  175.8 0.1 all_to_all.47
  175.9 0.1 copy.17
  175.9 12.4 %all_to_all.54 = bf16[4,8,1536]{2,0,1:T(4,128)(2,1)S(1)} all-to-all(bf16[4,8,1536]{2,0,1:T(4,128)(2,1)S(1)} %copy.17), channel_id=1, replica_groups=mesh['gx'=4,'yz'=8] {'yz'}, dimensions={1} | all-to-all | bytes 196608 | tf_op jit(solution)/shard_map/all_to_all | solution.py:85
  188.4 6.3 %all_gather.10 = bf16[128,1536]{1,0:T(8,128)(2,1)S(1)} all-gather(bf16[32,1536]{1,0:T(8,128)(2,1)S(1)} %all_to_all.50), channel_id=1, replica_groups=mesh['gx'=4,'yz'=8] {'gx'}, dimensions={0}, use_global_device_ids=true | all-gather | bytes 491520 | tf_op jit(solution)/shard_map/all_gather | solution.py:86
  194.7 9.1 %fusion.32 = f32[128,2304]{1,0:T(8,128)S(1)} fusion(bf16[128,4608]{1,0:T(8,128)(2,1)} %all-gather.2.cloned.1.call-done, bf16[4608,2304]{1,0:T(8,128)(2,1)} %param.17), kind=kOutput, calls=%fused_computation.42 | convolution fusion | flops 2717908992 | bytes 23592960 | tf_op jit(solution)/shard_map/dot_general | solution.py:97
  203.8 5.2 %convolution_add_fusion = f32[128,2304]{1,0:T(8,128)} fusion(f32[128,2304]{1,0:T(8,128)S(1)} %fusion.32, bf16[128,1536]{1,0:T(8,128)(2,1)S(1)} %all_gather.10, bf16[1536,2304]{1,0:T(8,128)(2,1)} %param.14), kind=kOutput, calls=%fused_computation | convolution fusion | flops 906264576 | bytes 9830400 | tf_op jit(solution)/shard_map/dot_general | solution.py:95
  209.0 61.2 %reduce-scatter.14.cloned.1.call-done = f32[16,2304]{1,0:T(8,128)} async-done(((f32[128,2304]{1,0:T(8,128)}), f32[16,2304]{1,0:T(8,128)}) %reduce-scatter.14.cloned.1.call-update) | async-done | bytes 147472 | tf_op jit(solution)/shard_map/reduce_scatter | solution.py:96
  270.2 1.6 convert_element_type.47
  (17 shorter events, 0.1 us)
Async XLA Ops:
  6.5 43.0 %copy-start = (bf16[2304,64]{0,1:T(8,128)(2,1)S(1)}, bf16[2304,64]{0,1:T(8,128)(2,1)}, u32[]{:S(2)}) copy-start(bf16[2304,64]{0,1:T(8,128)(2,1)} %param.13) | copy-start | bytes 884740
  6.5 72.0 %reduce-scatter.8.cloned.1.call-start = ((), (), s32[]{:S(2)}) async-start(), calls=%async_computation.9 | async-start | bytes 81920 | tf_op jit(solution)/shard_map/reduce_scatter | solution.py:74
  50.5 45.6 %reduce-scatter.6.cloned.1.call-start = ((), (), s32[]{:S(2)}) async-start(), calls=%async_computation.8 | async-start | bytes 983040 | tf_op jit(solution)/shard_map/reduce_scatter | solution.py:73
  55.6 76.2 %reduce-scatter.12.cloned.1.call-start = ((), (), s32[]{:S(2)}) async-start(), calls=%async_computation.11 | async-start | bytes 2949120 | tf_op jit(solution)/shard_map/reduce_scatter | solution.py:91
  67.1 100.4 %reduce-scatter.10.cloned.1.call-start = ((), (), s32[]{:S(2)}) async-start(), calls=%async_computation.10 | async-start | bytes 2949120 | tf_op jit(solution)/shard_map/reduce_scatter | solution.py:90
  78.5 6.8 %copy-start.2 = (s32[4]{0:T(128)S(1)}, s32[4]{0:T(128)}, u32[]{:S(2)}) copy-start(s32[4]{0:T(128)} %param.19) | copy-start | bytes 52
  80.0 11.8 %all-to-all-start.1 = ((bf16[8,2,128]{2,1,0:T(2,128)(2,1)}), bf16[8,2,128]{2,1,0:T(2,128)(2,1)S(1)}, u32[]{:S(2)}, u32[]{:S(2)}) async-start(bf16[8,2,128]{2,1,0:T(2,128)(2,1)} %reshape.47), calls=%async_computation.3 | async-start | bytes 8192 | tf_op jit(solution)/shard_map/all_to_all | solution.py:80
  97.7 12.6 %all-to-all-start = ((bf16[8,4,1536]{2,1,0:T(4,128)(2,1)}), bf16[8,4,1536]{2,1,0:T(4,128)(2,1)S(1)}, u32[]{:S(2)}, u32[]{:S(2)}) async-start(bf16[8,4,1536]{2,1,0:T(4,128)(2,1)} %all_to_all.40), calls=%async_computation.1 | async-start | bytes 196608 | tf_op jit(solution)/shard_map/all_to_all | solution.py:77
  103.2 91.5 %all-gather.2.cloned.1.call-start = ((), (), s32[]{:S(2)}) async-start(), calls=%async_computation.12 | async-start | bytes 1474560 | tf_op jit(solution)/shard_map/all_gather | solution.py:94
  169.6 100.5 %reduce-scatter.14.cloned.1.call-start = ((), (), s32[]{:S(2)}) async-start(), calls=%async_computation.13 | async-start | bytes 1327104 | tf_op jit(solution)/shard_map/reduce_scatter | solution.py:96
  203.8 67.9 %copy-start.1 = (bf16[2304,64]{0,1:T(8,128)(2,1)S(1)}, bf16[2304,64]{0,1:T(8,128)(2,1)}, u32[]{:S(2)}) copy-start(bf16[2304,64]{0,1:T(8,128)(2,1)} %param.13) | copy-start | bytes 884740
Sparse Core Ops, SparseCore 0:
  50.6 19.4 reduce-scatter.7
  72.8 23.2 reduce-scatter.5
  98.7 33.1 reduce-scatter.11
  134.4 33.0 reduce-scatter.9
  169.8 17.4 all-gather.1
  209.1 61.0 reduce-scatter.13
where the time goes:
time: 279 us
  waiting for transfers between devices  136 us (49%)
  blocking collectives  59.1 us (21%)
  matrix products  48.8 us (17%)
  between operations  13.6 us (5%)
  starting transfers between devices  11.1 us (4%)
  other arithmetic  8.58 us (3%)
    reduce_scatter x1, waiting for transfers between devices, body(): lax.psum_scatter(first + jnp.dot(hidden, down_weight, preferred_element_t...  61.2 us
    reduce_scatter x1, waiting for transfers between devices, body(): lax.psum_scatter(gate_part, 'gx', scatter_dimension=0, tiled=True)  35.7 us
    all_gather x1, blocking collectives, body(): gathered = lax.all_gather(normed, 'yz', axis=0, tiled=True)  32 us
    reduce_scatter x1, waiting for transfers between devices, body(): lax.psum_scatter(up_part, 'gx', scatter_dimension=0, tiled=True)  21.2 us
    all_to_all x1, blocking collectives, body(): lax.all_to_all(attended, 'yz', split_axis=1, concat_axis=0, tiled=True)  12.4 us
    dot_general x1, matrix products, body(): up_part = jnp.dot(gathered, up_weight, preferred_element_type=jnp.float32)  11.4 us
    dot_general x1, matrix products, body(): jnp.dot(gathered, gate_weight, preferred_element_type=jnp.float32)  11.4 us
    dot_general x1, matrix products, body(): jnp.dot(hidden, down_weight, preferred_element_type=jnp.float32)  9.09 us
  transfers between devices with their start and end apart: 8, of which 6 were waited for; matrix products, arithmetic and copies ran while one was open for 13% of the time, Pallas kernels for 0%

commit v1 on v0

--- a/solution.py
+++ b/solution.py
@@ -5,6 +5,32 @@
 from jax.sharding import PartitionSpec as P
 
 D = 9216
+
+
+def _handle_loads(row_data, array_axis):
+    row_data = jnp.moveaxis(row_data, 0, array_axis)
+    after = row_data.shape
+    return row_data.reshape(
+        *after[:array_axis], after[array_axis] * after[array_axis + 1], *after[array_axis + 2 :]
+    )
+
+
+def track_row(sample, net_axis):
+    nd = lax.axis_size(net_axis)
+    front = sample[None]
+    for pp in range(nd.bit_length() - 1):
+        p_next = 1 << pp
+        f_now = lax.ppermute(front, net_axis, [(ii, ii ^ p_next) for ii in range(nd)])
+        x_new = jnp.stack([front, f_now])
+        tile_out = lax.axis_index(net_axis)
+        now = tile_out >> pp & 1
+        front = jnp.where(now == 0, x_new, x_new[::-1]).reshape(-1, *sample.shape)
+    return front
+
+
+def _link_axis_part(s0, local_values, dim_k):
+    seen_now = track_row(s0, local_values)
+    return _handle_loads(seen_now, dim_k)
 
 
 def attend_local(query, new_kv, cache, lengths):
@@ -83,7 +109,7 @@
     )
     attended = attend_local(query_own, kv_own, cache, lengths)
     head_block = lax.all_to_all(attended, "yz", split_axis=1, concat_axis=0, tiled=True)
-    head_all = lax.all_gather(head_block, "gx", axis=0, tiled=True)
+    head_all = _link_axis_part(head_block, "gx", 0)
     gate_part = jnp.dot(gathered, gate_weight, preferred_element_type=jnp.float32)
     up_part = jnp.dot(gathered, up_weight, preferred_element_type=jnp.float32)
     gate_share, up_share = (

time: 279 us -> 275 us (0.986)
  blocking collectives: 59.1 us -> 40.3 us
  waiting for transfers between devices: 136 us -> 145 us
  starting transfers between devices: 11.1 us -> 15.1 us
    all_to_all x1 -> x0, blocking collectives: 12.4 us -> none  [body(): lax.all_to_all(attended, 'yz', split_axis=1, concat_axis=0, tiled=True)]
    reduce_scatter x1, waiting for transfers between devices: 21.2 us -> 10.9 us  [body(): lax.psum_scatter(up_part, 'gx', scatter_dimension=0, tiled=True)]
    all_gather x1, waiting for transfers between devices: 0.01 us -> 8.77 us  [body(): hidden = lax.all_gather(hidden_share, 'gx', axis=0, tiled=True)]
    ppermute x0 -> x2, waiting for transfers between devices: none -> 7.89 us  [track_row(): lax.ppermute(front, net_axis, [(ii, ii ^ p_next) for ii in range(nd)])]
    all_gather x1 -> x0, blocking collectives: 6.33 us -> none  [body(): head_all = lax.all_gather(head_block, 'gx', axis=0, tiled=True)]
    all_to_all x0 -> x1, starting transfers between devices: none -> 3.36 us  [body(): lax.all_to_all(attended, 'yz', split_axis=1, concat_axis=0, tiled=True)]
    reduce_scatter x1, waiting for transfers between devices: 61.2 us -> 64.3 us  [body(): lax.psum_scatter(first + jnp.dot(hidden, down_weight, preferred_element_t...]
  transfers between devices with their start and end apart: 8 -> 11, of which waited for: 6 -> 9; matrix products, arithmetic and copies ran while one was open for 13% -> 14% of each run, Pallas kernels for 0% -> 0%
where the time goes in v1:
time: 275 us; the launch traced here: 274 us
  waiting for transfers between devices  145 us (53%)
  matrix products  48.8 us (18%)
  blocking collectives  40.3 us (15%)
  starting transfers between devices  15.1 us (5%)
  between operations  13.6 us (5%)
  other arithmetic  8.76 us (3%)
    reduce_scatter x1, waiting for transfers between devices, body(): lax.psum_scatter(first + jnp.dot(hidden, down_weight, preferred_element_t...  64.3 us
    reduce_scatter x1, waiting for transfers between devices, body(): lax.psum_scatter(gate_part, 'gx', scatter_dimension=0, tiled=True)  35.7 us
    all_gather x1, blocking collectives, body(): gathered = lax.all_gather(normed, 'yz', axis=0, tiled=True)  32 us
    dot_general x1, matrix products, body(): up_part = jnp.dot(gathered, up_weight, preferred_element_type=jnp.float32)  11.4 us
    dot_general x1, matrix products, body(): jnp.dot(gathered, gate_weight, preferred_element_type=jnp.float32)  11.4 us
    reduce_scatter x1, waiting for transfers between devices, body(): lax.psum_scatter(up_part, 'gx', scatter_dimension=0, tiled=True)  10.9 us
    dot_general x1, matrix products, body(): jnp.dot(hidden, down_weight, preferred_element_type=jnp.float32)  9.09 us
    all_gather x1, waiting for transfers between devices, body(): hidden = lax.all_gather(hidden_share, 'gx', axis=0, tiled=True)  8.77 us
  transfers between devices with their start and end apart: 11, of which 9 were waited for; matrix products, arithmetic and copies ran while one was open for 14% of the time, Pallas kernels for 0%

profile of v1, /device:TPU:0, one launch (start us, length us, event | category | flops | bytes accessed | tf_op | source)
XLA Modules:
  0.0 274.3 jit_solution(15994826065642661938)
XLA Ops:
  6.5 1.1 convert_reduce_fusion
  7.6 0.7 convert_element_type.37
  8.3 8.3 %all-reduce = (f32[16]{0:T(128)S(1)}, f32[16]{0:T(128)S(1)}) all-reduce(f32[16]{0:T(128)S(1)} %get-tuple-element.6, f32[16]{0:T(128)S(1)} %get-tuple-element.5), channel_id=1, replica_groups=mesh['gx'=4,'yz'=8] {'gx'}, use_global_device_ids=true, to_apply=%region_3.0 | all-reduce | flops 32 | bytes 256 | tf_op jit(solution)/shard_map/psum | solution.py:85
  16.6 1.0 fusion.22
  17.6 32.0 %all_gather.6 = bf16[128,2304]{1,0:T(8,128)(2,1)S(1)} all-gather(bf16[16,2304]{1,0:T(8,128)(2,1)S(1)} %fusion.22), channel_id=1, replica_groups=mesh['gx'=4,'yz'=8] {'yz'}, dimensions={0}, use_global_device_ids=true | all-gather | bytes 663552 | tf_op jit(solution)/shard_map/all_gather | solution.py:95
  49.6 0.9 fusion.31
  50.5 0.0 reduce-scatter.6.cloned.1.call-start
  50.6 5.0 %fusion.30 = f32[128,1536]{1,0:T(8,128)} fusion(bf16[128,2304]{1,0:T(8,128)(2,1)S(1)} %all_gather.6, bf16[2304,1536]{1,0:T(8,128)(2,1)} %param.12), kind=kOutput, calls=%fused_computation.44 | convolution fusion | flops 905969664 | bytes 8454144 | tf_op jit(solution)/shard_map/dot_general | solution.py:96
  55.6 0.0 reduce-scatter.12.cloned.1.call-start
  55.7 11.4 %fusion.33 = f32[128,4608]{1,0:T(8,128)} fusion(bf16[128,2304]{1,0:T(8,128)(2,1)S(1)} %all_gather.6, bf16[2304,4608]{1,0:T(8,128)(2,1)} %param.16), kind=kOutput, calls=%fused_computation.47 | convolution fusion | flops 2717908992 | bytes 24182784 | tf_op jit(solution)/shard_map/dot_general | solution.py:114
  67.1 0.0 reduce-scatter.10.cloned.1.call-start
  67.2 11.4 %fusion.32 = f32[128,4608]{1,0:T(8,128)} fusion(bf16[128,2304]{1,0:T(8,128)(2,1)S(1)} %all_gather.6, bf16[2304,4608]{1,0:T(8,128)(2,1)} %param.15), kind=kOutput, calls=%fused_computation.46 | convolution fusion | flops 2717908992 | bytes 24182784 | tf_op jit(solution)/shard_map/dot_general | solution.py:113
  78.6 0.0 reduce-scatter.8.cloned.1.call-done
  78.6 0.7 convert_element_type.40
  79.3 0.7 reshape.53
  80.0 5.4 %all-to-all-start.1 = ((bf16[8,2,128]{2,1,0:T(2,128)(2,1)}), bf16[8,2,128]{2,1,0:T(2,128)(2,1)S(1)}, u32[]{:S(2)}, u32[]{:S(2)}) async-start(bf16[8,2,128]{2,1,0:T(2,128)(2,1)} %reshape.53), calls=%async_computation.3 | async-start | bytes 8192 | tf_op jit(solution)/shard_map/all_to_all | solution.py:106
  85.4 0.1 iota_compare_fusion
  85.5 6.3 %all-to-all-done.1 = bf16[8,2,128]{2,1,0:T(2,128)(2,1)S(1)} async-done(((bf16[8,2,128]{2,1,0:T(2,128)(2,1)}), bf16[8,2,128]{2,1,0:T(2,128)(2,1)S(1)}, u32[]{:S(2)}, u32[]{:S(2)}) %all-to-all-start.1) | async-done | bytes 4128 | tf_op jit(solution)/shard_map/all_to_all | solution.py:106
  91.8 0.1 reshape.54
  91.9 0.1 all_to_all.44
  91.9 4.2 %reduce-scatter.6.cloned.1.call-done = f32[32,1536]{1,0:T(8,128)} async-done(((f32[128,1536]{1,0:T(8,128)}), f32[32,1536]{1,0:T(8,128)}) %reduce-scatter.6.cloned.1.call-update) | async-done | bytes 196624 | tf_op jit(solution)/shard_map/reduce_scatter | solution.py:99
  96.1 0.9 convert_element_type.39
  97.1 0.7 all_to_all.38
  97.7 5.5 %all-to-all-start = ((bf16[8,4,1536]{2,1,0:T(4,128)(2,1)}), bf16[8,4,1536]{2,1,0:T(4,128)(2,1)S(1)}, u32[]{:S(2)}, u32[]{:S(2)}) async-start(bf16[8,4,1536]{2,1,0:T(4,128)(2,1)} %all_to_all.38), calls=%async_computation.1 | async-start | bytes 196608 | tf_op jit(solution)/shard_map/all_to_all | solution.py:103
  103.2 7.1 %all-to-all-done = bf16[8,4,1536]{2,1,0:T(4,128)(2,1)S(1)} async-done(((bf16[8,4,1536]{2,1,0:T(4,128)(2,1)}), bf16[8,4,1536]{2,1,0:T(4,128)(2,1)S(1)}, u32[]{:S(2)}, u32[]{:S(2)}) %all-to-all-start) | async-done | bytes 98336 | tf_op jit(solution)/shard_map/all_to_all | solution.py:103
  110.4 0.1 reshape.49
  110.5 0.1 fusion.24
  110.6 3.0 %select_reduce_fusion = (f32[4,48]{1,0:T(4,128)S(1)}, f32[4,48,1536]{2,1,0:T(8,128)S(1)}) fusion(f32[4,48]{1,0:T(4,128)S(1)} %broadcast_multiply_fusion, pred[4,1536]{1,0:T(4,128)(4,1)S(1)} %iota_compare_fusion, bf16[4,48,256]{2,1,0:T(8,128)(2,1)S(1)} %reshape.49, bf16[4,1536,512]{2,1,0:T(8,128)(2,1)} %param.18), kind=kOutput, calls=%fused_computation.8 | convolution fusion | flops 151879488 | bytes 4431360 | tf_op jit(solution)/shard_map/tgb,twb->tgw/dot_general | solution.py:47
  113.7 0.4 fusion.13
  114.1 2.6 fusion.10
  116.7 0.1 all_to_all.45
  116.8 0.7 copy.17
  117.5 3.4 %all-to-all-start.2 = ((bf16[4,8,1536]{2,0,1:T(4,128)(2,1)}), bf16[4,8,1536]{2,0,1:T(4,128)(2,1)S(1)}, u32[]{:S(2)}, u32[]{:S(2)}) async-start(bf16[4,8,1536]{2,0,1:T(4,128)(2,1)} %copy.17), calls=%async_computation.4 | async-start | bytes 196608 | tf_op jit(solution)/shard_map/all_to_all | solution.py:111
  120.9 0.0 all-gather.2.cloned.1.call-start
  120.9 10.9 %reduce-scatter.12.cloned.1.call-done = f32[32,4608]{1,0:T(8,128)} async-done(((f32[128,4608]{1,0:T(8,128)}), f32[32,4608]{1,0:T(8,128)}) %reduce-scatter.12.cloned.1.call-update) | async-done | bytes 589840 | tf_op jit(solution)/shard_map/reduce_scatter | solution.py:117
  131.8 35.7 %reduce-scatter.10.cloned.1.call-done = f32[32,4608]{1,0:T(8,128)} async-done(((f32[128,4608]{1,0:T(8,128)}), f32[32,4608]{1,0:T(8,128)}) %reduce-scatter.10.cloned.1.call-update) | async-done | bytes 589840 | tf_op jit(solution)/shard_map/reduce_scatter | solution.py:116
  167.5 2.1 multiply_convert_fusion
  169.7 0.2 reduce-scatter.14.cloned.1.call-start
  169.9 0.1 collective-permute-start
  170.1 1.2 collective-permute-done
  171.4 0.4 collective-permute-start.1
  171.8 6.6 %collective-permute-done.1 = bf16[2,32,1536]{2,1,0:T(8,128)(2,1)S(1)} collective-permute-done((bf16[2,32,1536]{2,1,0:T(8,128)(2,1)S(1)}, bf16[2,32,1536]{2,1,0:T(8,128)(2,1)S(1)}, u32[]{:S(2)}, u32[]{:S(2)}) %collective-permute-start.1) | collective-permute-done | bytes 196640 | tf_op jit(solution)/shard_map/ppermute | solution.py:23
  178.4 0.1 reverse_select_fusion
  178.5 8.8 %all-gather.2.cloned.1.call-done = bf16[128,4608]{1,0:T(8,128)(2,1)} async-done(((bf16[32,4608]{1,0:T(8,128)(2,1)}), bf16[128,4608]{1,0:T(8,128)(2,1)}) %all-gather.2.cloned.1.call-update) | async-done | bytes 1179664 | tf_op jit(solution)/shard_map/all_gather | solution.py:120
  187.3 9.1 %fusion.34 = f32[128,2304]{1,0:T(8,128)S(1)} fusion(bf16[128,4608]{1,0:T(8,128)(2,1)} %all-gather.2.cloned.1.call-done, bf16[4608,2304]{1,0:T(8,128)(2,1)} %param.17), kind=kOutput, calls=%fused_computation.48 | convolution fusion | flops 2717908992 | bytes 23592960 | tf_op jit(solution)/shard_map/dot_general | solution.py:123
  196.4 5.2 %convolution_add_fusion = f32[128,2304]{1,0:T(8,128)} fusion(f32[128,2304]{1,0:T(8,128)S(1)} %fusion.34, bf16[128,1536]{1,0:T(8,128)(2,1)S(1)} %bitcast.29, bf16[1536,2304]{1,0:T(8,128)(2,1)} %param.14), kind=kOutput, calls=%fused_computation | convolution fusion | flops 906264576 | bytes 9830400 | tf_op jit(solution)/shard_map/dot_general | solution.py:121
  201.6 64.3 %reduce-scatter.14.cloned.1.call-done = f32[16,2304]{1,0:T(8,128)} async-done(((f32[128,2304]{1,0:T(8,128)}), f32[16,2304]{1,0:T(8,128)}) %reduce-scatter.14.cloned.1.call-update) | async-done | bytes 147472 | tf_op jit(solution)/shard_map/reduce_scatter | solution.py:122
  265.9 1.6 convert_element_type.47
  (26 shorter events, 0.3 us)
Async XLA Ops:
  6.5 43.0 %copy-start = (bf16[2304,64]{0,1:T(8,128)(2,1)S(1)}, bf16[2304,64]{0,1:T(8,128)(2,1)}, u32[]{:S(2)}) copy-start(bf16[2304,64]{0,1:T(8,128)(2,1)} %param.13) | copy-start | bytes 884740
  6.5 72.1 %reduce-scatter.8.cloned.1.call-start = ((), (), s32[]{:S(2)}) async-start(), calls=%async_computation.9 | async-start | bytes 81920 | tf_op jit(solution)/shard_map/reduce_scatter | solution.py:100
  50.5 45.6 %reduce-scatter.6.cloned.1.call-start = ((), (), s32[]{:S(2)}) async-start(), calls=%async_computation.8 | async-start | bytes 983040 | tf_op jit(solution)/shard_map/reduce_scatter | solution.py:99
  55.6 76.2 %reduce-scatter.12.cloned.1.call-start = ((), (), s32[]{:S(2)}) async-start(), calls=%async_computation.11 | async-start | bytes 2949120 | tf_op jit(solution)/shard_map/reduce_scatter | solution.py:117
  67.1 100.4 %reduce-scatter.10.cloned.1.call-start = ((), (), s32[]{:S(2)}) async-start(), calls=%async_computation.10 | async-start | bytes 2949120 | tf_op jit(solution)/shard_map/reduce_scatter | solution.py:116
  78.6 6.8 %copy-start.2 = (s32[4]{0:T(128)S(1)}, s32[4]{0:T(128)}, u32[]{:S(2)}) copy-start(s32[4]{0:T(128)} %param.19) | copy-start | bytes 52
  80.0 11.8 %all-to-all-start.1 = ((bf16[8,2,128]{2,1,0:T(2,128)(2,1)}), bf16[8,2,128]{2,1,0:T(2,128)(2,1)S(1)}, u32[]{:S(2)}, u32[]{:S(2)}) async-start(bf16[8,2,128]{2,1,0:T(2,128)(2,1)} %reshape.53), calls=%async_computation.3 | async-start | bytes 8192 | tf_op jit(solution)/shard_map/all_to_all | solution.py:106
  97.7 12.6 %all-to-all-start = ((bf16[8,4,1536]{2,1,0:T(4,128)(2,1)}), bf16[8,4,1536]{2,1,0:T(4,128)(2,1)S(1)}, u32[]{:S(2)}, u32[]{:S(2)}) async-start(bf16[8,4,1536]{2,1,0:T(4,128)(2,1)} %all_to_all.38), calls=%async_computation.1 | async-start | bytes 196608 | tf_op jit(solution)/shard_map/all_to_all | solution.py:103
  117.5 52.4 %all-to-all-start.2 = ((bf16[4,8,1536]{2,0,1:T(4,128)(2,1)}), bf16[4,8,1536]{2,0,1:T(4,128)(2,1)S(1)}, u32[]{:S(2)}, u32[]{:S(2)}) async-start(bf16[4,8,1536]{2,0,1:T(4,128)(2,1)} %copy.17), calls=%async_computation.4 | async-start | bytes 196608 | tf_op jit(solution)/shard_map/all_to_all | solution.py:111
  120.9 66.4 %all-gather.2.cloned.1.call-start = ((), (), s32[]{:S(2)}) async-start(), calls=%async_computation.12 | async-start | bytes 1474560 | tf_op jit(solution)/shard_map/all_gather | solution.py:120
  169.7 96.3 %reduce-scatter.14.cloned.1.call-start = ((), (), s32[]{:S(2)}) async-start(), calls=%async_computation.13 | async-start | bytes 1327104 | tf_op jit(solution)/shard_map/reduce_scatter | solution.py:122
  169.9 1.4 collective-permute-start
  171.4 7.0 %collective-permute-start.1 = (bf16[2,32,1536]{2,1,0:T(8,128)(2,1)S(1)}, bf16[2,32,1536]{2,1,0:T(8,128)(2,1)S(1)}, u32[]{:S(2)}, u32[]{:S(2)}) collective-permute-start(bf16[2,32,1536]{2,1,0:T(8,128)(2,1)S(1)} %get-tuple-element.10), channel_id=1, source_target_pairs={{0,16},{8,24},{16,0},{24,8},{1,17},{9,25},{17,1},{25,9},{2,18},{10... | collective-permute-start | bytes 589832 | tf_op jit(solution)/shard_map/ppermute | solution.py:23
  196.4 71.1 %copy-start.1 = (bf16[2304,64]{0,1:T(8,128)(2,1)S(1)}, bf16[2304,64]{0,1:T(8,128)(2,1)}, u32[]{:S(2)}) copy-start(bf16[2304,64]{0,1:T(8,128)(2,1)} %param.13) | copy-start | bytes 884740
Sparse Core Ops, SparseCore 0:
  50.6 19.4 reduce-scatter.7
  72.8 23.2 reduce-scatter.5
  98.7 33.1 reduce-scatter.11
  134.4 33.0 reduce-scatter.9
  169.8 17.4 all-gather.1
  201.7 64.1 reduce-scatter.13
